TPU v7x, 32 devices: a whole 2x2x4 slice. The times are simulated.
32 devices in a mesh: section: 2 (over x), seq: 16 (over z, y, core).
Axes of the slice: x: 2, y: 2, z: 4, core: 2. Of those that a mesh axis runs over, the one named last changes fastest.
Arguments:
- section_input: bfloat16 [2, 2, 2048, 2048], P('section', None, 'seq'), may hold values from -6 to 6
- out_grad: bfloat16 [2, 2048, 2048], P(None, 'seq'), may hold values from -6 to 6
- norm_gain: float32 [2, 2048], P('section'), may hold values from 0.1 to 1.9
- query_weight: bfloat16 [2, 2048, 1024], P('section', 'seq'), may hold values from -0.125 to 0.125
- output_weight: bfloat16 [2, 1024, 2048], P('section', 'seq'), may hold values from -0.1875 to 0.1875
- header_keys: bfloat16 [2, 2, 64, 256], P('section', None, 'seq'), may hold values from -6 to 6
- header_values: bfloat16 [2, 2, 64, 256], P('section', None, 'seq'), may hold values from -6 to 6
- header_pos: int32 [2, 64], replicated, may hold values from 0 to 2047
- segment_ids: int32 [2, 2048], P(None, 'seq'), may hold values from 0 to 7, never falling along the last dimension, each value on 1 to 512 neighbouring positions
Outputs:
- grad_input: bfloat16 [2, 2, 2048, 2048], P('section', None, 'seq')
- header_key_gradient: float32 [2, 2, 64, 256], P('section', None, 'seq')
- header_value_gradient: float32 [2, 2, 64, 256], P('section', None, 'seq')
Inputs may be any that keep to these rules, and one draw needn't show every extreme that they name: `segment_ids`: ids never fall along a sheet's cells; every id occurs, and no id covers more than 512 cells.
All inputs are finite; a program needn't handle non-finite values.
Results may differ from a plain program's by a relative error of at most 0.0085.
Values may be sent and summed in bfloat16 or wider, within the bound.
A program may use at most 64 MiB of HBM per device.

v0:
```python
import math

import jax
import jax.numpy as jnp
from jax import lax
from jax.sharding import PartitionSpec as P

KEY_HEADS = 4
HEAD_WIDTH = 64
HPS = 8


EPSILON = 1e-05
ROPE_BASE = 500000.0


def shifted(value, axis, steps):
    count = lax.axis_size(axis)
    initial, last = (max(0, -steps), min(count, count - steps))
    return lax.ppermute(value, axis, [(source, source + steps) for source in range(initial, last)])


def rope_tables(positions, half_width):
    freq_index = jnp.arange(half_width, dtype=jnp.float32)
    inverse = jnp.exp(freq_index * (-2.0 * math.log(ROPE_BASE) / (2 * half_width)))
    angles = positions.astype(jnp.float32)[..., None] * inverse
    return (jnp.cos(angles), jnp.sin(angles))


def apply_rotary(vectors, cosine, sine_part):
    half_width = vectors.shape[-1] // 2
    first_half = vectors[..., :half_width]
    second = vectors[..., half_width:]
    cos_wide = cosine[..., None, :]
    sin_wide = sine_part[..., None, :]
    return jnp.concatenate(
        [first_half * cos_wide - second * sin_wide, second * cos_wide + first_half * sin_wide],
        axis=-1,
    )


def forward_probs(
    section_rows, norm_scale, query_full, keys_rotated, allowed, cell_cosine, cell_sine
):
    cell_number = section_rows.shape[0]
    kv_heads = keys_rotated.shape[1]
    head_size = keys_rotated.shape[2]
    q_heads = query_full.shape[1] // head_size
    widened = section_rows.astype(jnp.float32)
    inv_rms = lax.rsqrt(jnp.mean(widened * widened, axis=-1, keepdims=True) + EPSILON)
    normed = (widened * inv_rms * norm_scale).astype(jnp.bfloat16)
    projected_rows = jnp.dot(normed, query_full, preferred_element_type=jnp.float32)
    query_matrix = apply_rotary(
        projected_rows.reshape(cell_number, q_heads, head_size), cell_cosine, cell_sine
    ).astype(jnp.bfloat16)
    query_matrix = query_matrix.reshape(cell_number, kv_heads, q_heads // kv_heads, head_size)
    scores = jnp.einsum(
        "ngjd,kgd->gjnk", query_matrix, keys_rotated, preferred_element_type=jnp.float32
    ) * head_size ** (-0.5)
    weights_exp = jnp.exp(scores) * allowed
    probabilities = (weights_exp / jnp.sum(weights_exp, axis=-1, keepdims=True)).astype(
        jnp.bfloat16
    )
    return (inv_rms, query_matrix, probabilities)


def backward_rows(
    section_rows,
    norm_scale,
    inv_rms,
    query_matrix,
    probabilities,
    grad_output,
    query_full,
    output_full,
    keys_rotated,
    header_value_rows,
    cell_cosine,
    cell_sine,
):
    cell_number, kv_heads, group_size, head_size = query_matrix.shape
    widened = section_rows.astype(jnp.float32)
    head_gradients = jnp.einsum(
        "nd,qd->nq", grad_output, output_full, preferred_element_type=jnp.float32
    ).astype(jnp.bfloat16)
    head_gradients = head_gradients.reshape(cell_number, kv_heads, group_size, head_size)
    grad_probs = jnp.einsum(
        "ngjd,kgd->gjnk", head_gradients, header_value_rows, preferred_element_type=jnp.float32
    )
    broad_probs = probabilities.astype(jnp.float32)
    row_total = jnp.sum(broad_probs * grad_probs, axis=-1, keepdims=True)
    grad_scores = (broad_probs * (grad_probs - row_total) * head_size ** (-0.5)).astype(
        jnp.bfloat16
    )
    grad_rot = jnp.einsum(
        "gjnk,kgd->ngjd", grad_scores, keys_rotated, preferred_element_type=jnp.float32
    )
    grad_rot = grad_rot.reshape(cell_number, kv_heads * group_size, head_size)
    grad_query = (
        apply_rotary(grad_rot, cell_cosine, -cell_sine)
        .astype(jnp.bfloat16)
        .reshape(cell_number, -1)
    )
    grad_normed = jnp.einsum(
        "nq,dq->nd", grad_query, query_full, preferred_element_type=jnp.float32
    )
    scaled = grad_normed * norm_scale
    grad_input = (
        grad_output.astype(jnp.float32)
        + inv_rms * scaled
        - widened * inv_rms**3 * jnp.mean(widened * scaled, axis=-1, keepdims=True)
    )
    key_rotated = jnp.einsum(
        "uohb,huox->bux", grad_scores, query_matrix, preferred_element_type=jnp.float32
    )
    value_part = jnp.einsum(
        "uohb,huox->bux", probabilities, head_gradients, preferred_element_type=jnp.float32
    )
    total_heads = key_rotated.shape[0]
    return (
        grad_input.astype(jnp.bfloat16),
        key_rotated.reshape(total_heads, kv_heads * head_size),
        value_part.reshape(total_heads, kv_heads * head_size),
    )


def per_device(
    section_input,
    out_grad,
    norm_gain,
    query_weight,
    output_weight,
    header_keys,
    header_values,
    header_pos,
    segment_ids,
):
    sections = lax.axis_size("section")
    section_here = lax.axis_index("section")
    seq_here = lax.axis_index("seq")
    microbatch = section_input.shape[1]
    cell_number = section_input.shape[2]
    width = section_input.shape[3]
    pieces = 1
    rows_each = cell_number // pieces
    item_count = microbatch * pieces
    norm_scale = norm_gain[0]
    every_key, every_value = (
        lax.all_gather(header_keys[0], "seq", axis=1, tiled=True),
        lax.all_gather(header_values[0], "seq", axis=1, tiled=True),
    )
    total_heads = every_key.shape[1]
    header_cosine, header_sine = rope_tables(header_pos, HEAD_WIDTH // 2)
    keys_rotated = apply_rotary(
        every_key.astype(jnp.float32).reshape(microbatch, total_heads, KEY_HEADS, HEAD_WIDTH),
        header_cosine,
        header_sine,
    ).astype(jnp.bfloat16)
    header_value_rows = every_value.reshape(microbatch, total_heads, KEY_HEADS, HEAD_WIDTH)
    positions = seq_here * cell_number + jnp.arange(cell_number, dtype=jnp.int32)
    cell_cosine, cell_sine = rope_tables(positions, HEAD_WIDTH // 2)
    cos_items = cell_cosine.reshape(pieces, rows_each, -1)
    sin_items = cell_sine.reshape(pieces, rows_each, -1)
    header_segment = jnp.arange(total_heads, dtype=jnp.int32) // HPS
    allowed = (segment_ids[:, :, None] == header_segment[None, None, :]).astype(jnp.float32)
    section_items = section_input[0]
    query_full, output_full = (
        lax.all_gather(query_weight[0], "seq", axis=0, tiled=True),
        lax.all_gather(output_weight[0], "seq", axis=0, tiled=True),
    )

    def work(operand):
        item_index, grad_output = operand
        slot_index = item_index // pieces
        piece_index = item_index % pieces
        section_rows = lax.dynamic_index_in_dim(section_items, item_index, 0, keepdims=False)
        keys_now = lax.dynamic_index_in_dim(keys_rotated, slot_index, 0, keepdims=False)
        vals_now = lax.dynamic_index_in_dim(header_value_rows, slot_index, 0, keepdims=False)
        cos_now = lax.dynamic_index_in_dim(cos_items, piece_index, 0, keepdims=False)
        sin_now = lax.dynamic_index_in_dim(sin_items, piece_index, 0, keepdims=False)
        allowed_now = lax.dynamic_index_in_dim(allowed, item_index, 0, keepdims=False)
        inv_rms, query_matrix, probabilities = forward_probs(
            section_rows, norm_scale, query_full, keys_now, allowed_now, cos_now, sin_now
        )
        return backward_rows(
            section_rows,
            norm_scale,
            inv_rms,
            query_matrix,
            probabilities,
            grad_output,
            query_full,
            output_full,
            keys_now,
            vals_now,
            cos_now,
            sin_now,
        )

    def skipped(operand):
        return (
            jnp.zeros((rows_each, width), jnp.bfloat16),
            jnp.zeros((total_heads, KEY_HEADS * HEAD_WIDTH), jnp.float32),
            jnp.zeros((total_heads, KEY_HEADS * HEAD_WIDTH), jnp.float32),
        )

    def step(tick_index, carry):
        incoming, grads_out, key_acc, value_acc = carry
        item_now = tick_index - (sections - 1 - section_here)
        active = (item_now >= 0) & (item_now < item_count)
        item_index = jnp.clip(item_now, 0, item_count - 1)
        slot_index = item_index // pieces
        from_loss = lax.dynamic_index_in_dim(out_grad, item_index, 0, keepdims=False)
        grad_output = jnp.where(section_here == sections - 1, from_loss, incoming)
        grad_input, key_part, value_part = lax.cond(
            active, work, skipped, (item_index, grad_output)
        )
        previous = lax.dynamic_index_in_dim(grads_out, item_index, 0, keepdims=False)
        grads_out = lax.dynamic_update_index_in_dim(
            grads_out, jnp.where(active, grad_input, previous), item_index, 0
        )
        key_acc = key_acc.at[slot_index].add(key_part)
        value_acc = value_acc.at[slot_index].add(value_part)
        incoming = shifted(grad_input, "section", -1)
        return (incoming, grads_out, key_acc, value_acc)

    initial = (
        jnp.zeros((rows_each, width), jnp.bfloat16),
        jnp.zeros((item_count, rows_each, width), jnp.bfloat16),
        jnp.zeros((microbatch, total_heads, KEY_HEADS * HEAD_WIDTH), jnp.float32),
        jnp.zeros((microbatch, total_heads, KEY_HEADS * HEAD_WIDTH), jnp.float32),
    )
    final = lax.fori_loop(0, sections + item_count - 1, step, initial)
    key_total, value_sum = (
        lax.psum_scatter(final[2], "seq", scatter_dimension=1, tiled=True),
        lax.psum_scatter(final[3], "seq", scatter_dimension=1, tiled=True),
    )
    local_rows = key_total.shape[1]
    own_pos = lax.dynamic_slice_in_dim(header_pos, seq_here * local_rows, local_rows, 1)
    local_cosine, local_sine = rope_tables(own_pos, HEAD_WIDTH // 2)
    header_key_gradient = apply_rotary(
        key_total.reshape(microbatch, local_rows, KEY_HEADS, HEAD_WIDTH), local_cosine, -local_sine
    ).reshape(microbatch, local_rows, KEY_HEADS * HEAD_WIDTH)
    grads_all = final[1]
    return (grads_all[None], header_key_gradient[None], value_sum[None])


def solution(mesh):
    in_specs = (
        P("section", None, "seq", None),
        P(None, "seq", None),
        P("section", None),
        P("section", "seq", None),
        P("section", "seq", None),
        P("section", None, "seq", None),
        P("section", None, "seq", None),
        P(),
        P(None, "seq"),
    )
    out_specs = (
        P("section", None, "seq", None),
        P("section", None, "seq", None),
        P("section", None, "seq", None),
    )
    return jax.shard_map(
        per_device, mesh=mesh, in_specs=in_specs, out_specs=out_specs, check_vma=False
    )
```

profile of v0, /device:TPU:0, one launch (start us, length us, event | category | flops | bytes accessed | tf_op | source)
XLA Modules:
  0.0 321.8 jit_solution(15233449904454467029)
XLA Ops:
  7.2 1.9 copy.44
  11.3 23.4 %all-gather = bf16[1,2,64,256]{3,1,0,2:T(2,128)(2,1)S(1)} all-gather(bf16[1,2,4,256]{3,1,0,2:T(2,128)(2,1)S(1)} %copy.42), channel_id=2, replica_groups=mesh['section'=2,'seq'=16] {'seq'}, dimensions={2}, use_global_device_ids=true | all-gather | bytes 69632 | tf_op jit(solution)/shard_map/all_gather | solution.py:149
  37.0 18.1 %all-gather.2 = bf16[1,2,64,256]{3,1,0,2:T(2,128)(2,1)S(1)} all-gather(bf16[1,2,4,256]{3,1,0,2:T(2,128)(2,1)S(1)} %copy.45), channel_id=4, replica_groups=mesh['section'=2,'seq'=16] {'seq'}, dimensions={2}, use_global_device_ids=true | all-gather | bytes 69632 | tf_op jit(solution)/shard_map/all_gather | solution.py:150
  59.4 8.0 %all-gather.7.cloned.1.call-done = bf16[1,2048,1024]{1,2,0:T(8,128)(2,1)} async-done(((bf16[1,128,1024]{1,2,0:T(8,128)(2,1)}), bf16[1,2048,1024]{1,2,0:T(8,128)(2,1)}) %all-gather.7.cloned.1.call-update) | async-done | bytes 4194320 | tf_op jit(solution)/shard_map/all_gather | solution.py:168
  67.4 50.2 %all-gather.9.cloned.1.call-done = bf16[1,1024,2048]{2,1,0:T(8,128)(2,1)} async-done(((bf16[1,64,2048]{2,1,0:T(8,128)(2,1)}), bf16[1,1024,2048]{2,1,0:T(8,128)(2,1)}) %all-gather.9.cloned.1.call-update) | async-done | bytes 4194320 | tf_op jit(solution)/shard_map/all_gather | solution.py:169
  120.1 105.4 %while.25 = (s32[]{:T(128)}, bf16[128,2048]{1,0:T(8,128)(2,1)S(1)}, bf16[2,128,2048]{2,1,0:T(8,128)(2,1)}, f32[2,64,256]{2,0,1:T(2,128)}, f32[2,64,256]{2,1,0:T(...) while((s32[]{:T(128)}, bf16[128,2048]{1,0:T(8,128)(2,1)S(1)}, ...), condition=%wide.region_8.9_spmd.clone.clone, body=%wide.region_0.8_spmd.clone.clone.sunk | while | flops 1723318784 | bytes 35277956 | solution.py:233
  124.2 1.5 and_reduce_fusion.2
  128.2 2.3 scatter-add.18
  131.5 23.8 %collective-permute-done = bf16[128,2048]{1,0:T(8,128)(2,1)S(1)} collective-permute-done((bf16[128,2048]{1,0:T(8,128)(2,1)S(1)}, bf16[128,2048]{1,0:T(8,128)(2,1)S(1)}, u32[]{:S(2)}, u32[]{:S(2)}) %collective-permute-start) | collective-permute-done | bytes 524320 | tf_op jit(solution)/shard_map/while/body/eval_jaxpr/ppermute | solution.py:20
  155.9 19.4 %conditional.4 = (bf16[128,2048]{1,0:T(8,128)(2,1)S(1)}, f32[1,64,256]{1,2,0:T(8,128)S(1)}, f32[1,64,256]{1,2,0:T(8,128)S(1)}) conditional(s32[]{:T(128)} %convert_element_type.166, () %tuple.101, (pred[]{:T(512)}, bf16[2,128,2048]{2,1,0:T(8,128)(2,1)}, s32[]{:T(128)}, bf16[128,2048]{1,0:T(8,128)(2,1)S(1)}, bf16[2,128,2048]{2,1,0:T(8,128)(2,1)S(1)}, ...), branch_computations={%region_1.1_spmd, %region_2.6_spmd} | conditional | flops 1722954240 | bytes 29024924 | solution.py:215
  156.6 3.5 %fusion.35 = f32[128,16,64]{0,2,1:T(8,128)S(1)} fusion(bf16[16,64,2048]{2,1,0:T(8,128)(2,1)} %bitcast.131, f32[2048]{0:T(1024)S(1)} %bitcast.147, f32[128]{0:T(128)S(1)} %get-tuple-element.744, bf16[2,128,2048]{2,1,0:T(8,128)(2,1)S(1)} %get-tuple-element.506, s32[]{:T(128)S(6)} %select_n.99), kind=kOutput, calls=%fused_computation.35 | convolution fusion | flops 537919488 | bytes 5251588 | tf_op jit(solution)/shard_map/while/body/eval_jaxpr/cond/branch_1_fun/dot_general | solution.py:52
  160.4 1.9 divide_convert_fusion
  162.3 3.9 %convolution_convert_fusion = bf16[128,1024]{1,0:T(8,128)(2,1)S(1)} fusion(bf16[1024,2048]{1,0:T(8,128)(2,1)} %get-tuple-element.514, bf16[128,2048]{1,0:T(8,128)(2,1)S(1)} %get-tuple-element.505, bf16[2,128,2048]{2,1,0:T(8,128)(2,1)} %get-tuple-element.503, s32[]{:T(128)} %get-tuple-element.504, pred[]{:T(512)} %get-tuple-element.502), kind=kOutput, calls=%fused_computation.19 | convolution fusion | flops 537264128 | bytes 5506048 | tf_op jit(solution)/shard_map/while/body/eval_jaxpr/cond/branch_1_fun/nd,qd->nq/dot_general | solution.py:83
  166.5 1.3 fusion.17
  167.9 1.4 fusion.18
  169.5 3.0 fusion.23
  172.5 1.4 fusion.22
  178.6 1.5 and_reduce_fusion.2
  182.7 2.3 scatter-add.18
  185.9 4.9 %collective-permute-done = bf16[128,2048]{1,0:T(8,128)(2,1)S(1)} collective-permute-done((bf16[128,2048]{1,0:T(8,128)(2,1)S(1)}, bf16[128,2048]{1,0:T(8,128)(2,1)S(1)}, u32[]{:S(2)}, u32[]{:S(2)}) %collective-permute-start) | collective-permute-done | bytes 524320 | tf_op jit(solution)/shard_map/while/body/eval_jaxpr/ppermute | solution.py:20
  191.4 19.4 %conditional.4 = (bf16[128,2048]{1,0:T(8,128)(2,1)S(1)}, f32[1,64,256]{1,2,0:T(8,128)S(1)}, f32[1,64,256]{1,2,0:T(8,128)S(1)}) conditional(s32[]{:T(128)} %convert_element_type.166, () %tuple.101, (pred[]{:T(512)}, bf16[2,128,2048]{2,1,0:T(8,128)(2,1)}, s32[]{:T(128)}, bf16[128,2048]{1,0:T(8,128)(2,1)S(1)}, bf16[2,128,2048]{2,1,0:T(8,128)(2,1)S(1)}, ...), branch_computations={%region_1.1_spmd, %region_2.6_spmd} | conditional | flops 1722954240 | bytes 29024924 | solution.py:215
  192.2 3.5 %fusion.35 = f32[128,16,64]{0,2,1:T(8,128)S(1)} fusion(bf16[16,64,2048]{2,1,0:T(8,128)(2,1)} %bitcast.131, f32[2048]{0:T(1024)S(1)} %bitcast.147, f32[128]{0:T(128)S(1)} %get-tuple-element.744, bf16[2,128,2048]{2,1,0:T(8,128)(2,1)S(1)} %get-tuple-element.506, s32[]{:T(128)S(6)} %select_n.99), kind=kOutput, calls=%fused_computation.35 | convolution fusion | flops 537919488 | bytes 5251588 | tf_op jit(solution)/shard_map/while/body/eval_jaxpr/cond/branch_1_fun/dot_general | solution.py:52
  195.9 1.9 divide_convert_fusion
  197.8 3.9 %convolution_convert_fusion = bf16[128,1024]{1,0:T(8,128)(2,1)S(1)} fusion(bf16[1024,2048]{1,0:T(8,128)(2,1)} %get-tuple-element.514, bf16[128,2048]{1,0:T(8,128)(2,1)S(1)} %get-tuple-element.505, bf16[2,128,2048]{2,1,0:T(8,128)(2,1)} %get-tuple-element.503, s32[]{:T(128)} %get-tuple-element.504, pred[]{:T(512)} %get-tuple-element.502), kind=kOutput, calls=%fused_computation.19 | convolution fusion | flops 537264128 | bytes 5506048 | tf_op jit(solution)/shard_map/while/body/eval_jaxpr/cond/branch_1_fun/nd,qd->nq/dot_general | solution.py:83
  202.1 1.3 fusion.17
  203.5 1.4 fusion.18
  205.0 3.0 fusion.23
  208.1 1.4 fusion.22
  214.2 1.5 and_reduce_fusion.2
  218.3 2.3 scatter-add.18
  221.5 4.0 %collective-permute-done = bf16[128,2048]{1,0:T(8,128)(2,1)S(1)} collective-permute-done((bf16[128,2048]{1,0:T(8,128)(2,1)S(1)}, bf16[128,2048]{1,0:T(8,128)(2,1)S(1)}, u32[]{:S(2)}, u32[]{:S(2)}) %collective-permute-start) | collective-permute-done | bytes 524320 | tf_op jit(solution)/shard_map/while/body/eval_jaxpr/ppermute | solution.py:20
  226.3 85.9 %all-reduce.5.cloned.1.call-done = (f32[2,64,256]{2,0,1:T(2,128)}, f32[2,64,256]{2,1,0:T(8,128)}) async-done(((f32[2,64,256]{2,0,1:T(2,128)}, f32[2,64,256]{2,1,0:T(8,128)}), (f32[2,64,256]{2,0,1:T(2,128)}, f32[2,64,256]{2,1,0:T(8,128)})) %all-reduce.5.cloned.1.call-update) | async-done | bytes 262160
  (152 shorter events, 42.4 us)
Async XLA Ops:
  7.2 112.9 %copy-start = (bf16[1,2,128,2048]{3,2,1,0:T(8,128)(2,1)S(1)}, bf16[1,2,128,2048]{3,2,1,0:T(8,128)(2,1)}, u32[]{:S(2)}) copy-start(bf16[1,2,128,2048]{3,2,1,0:T(8,128)(2,1)} %param.17) | copy-start | bytes 3145732
  7.2 112.9 %copy-start.2 = (f32[1,2048]{1,0:T(1,128)S(1)}, f32[1,2048]{1,0:T(1,128)}, u32[]{:S(2)}) copy-start(f32[1,2048]{1,0:T(1,128)} %param.19) | copy-start | bytes 24580
  7.2 112.9 %copy-start.3 = (s32[2,128]{1,0:T(2,128)S(1)}, s32[2,128]{1,0:T(2,128)}, u32[]{:S(2)}) copy-start(s32[2,128]{1,0:T(2,128)} %param.25) | copy-start | bytes 3076
  7.2 60.2 %all-gather.7.cloned.1.call-start = ((), (), s32[]{:S(2)}) async-start(), calls=%async_computation | async-start | bytes 4456448 | tf_op jit(solution)/shard_map/all_gather | solution.py:168
  9.1 108.5 %all-gather.9.cloned.1.call-start = ((), (), s32[]{:S(2)}) async-start(), calls=%async_computation.1 | async-start | bytes 4456448 | tf_op jit(solution)/shard_map/all_gather | solution.py:169
  9.9 302.4 %all-reduce.5.cloned.1.call-start = ((), (), s32[]{:S(2)}) async-start(), calls=%async_computation.2 | async-start | bytes 524288
  120.1 0.6 copy-start.4
  120.1 0.6 copy-start.6
  120.1 0.6 copy-start.9
  120.8 34.4 %copy-start.5 = (f32[32]{0:T(128)S(1)}, f32[32]{0:T(128)}, u32[]{:S(2)}) copy-start(f32[32]{0:T(128)} %copy-done.4) | copy-start | bytes 388 | tf_op jit(solution)/shard_map/while
  120.8 34.4 %copy-start.7 = (s32[64]{0:T(128)S(1)}, s32[64]{0:T(128)}, u32[]{:S(2)}) copy-start(s32[64]{0:T(128)} %copy-done.6) | copy-start | bytes 772 | tf_op jit(solution)/shard_map/while
  120.8 34.4 %copy-start.10 = (f32[128]{0:T(128)S(1)}, f32[128]{0:T(128)}, u32[]{:S(2)}) copy-start(f32[128]{0:T(128)} %copy-done.9) | copy-start | bytes 1540 | tf_op jit(solution)/shard_map/while
  120.8 34.4 %collective-permute-start = (bf16[128,2048]{1,0:T(8,128)(2,1)S(1)}, bf16[128,2048]{1,0:T(8,128)(2,1)S(1)}, u32[]{:S(2)}, u32[]{:S(2)}) collective-permute-start(bf16[128,2048]{1,0:T(8,128)(2,1)S(1)} %get-tuple-element.873), channel_id=1, source_target_pairs={{16,0},{17,1},{18,2},{19,3},{20,4},{21,5},{22,6},{23,7},{24,8},{25... | collective-permute-start | bytes 1572872 | tf_op jit(solution)/shard_map/while/body/eval_jaxpr/ppermute | solution.py:20
  155.3 0.6 copy-start.4
  155.3 0.6 copy-start.6
  155.3 0.6 copy-start.9
  160.4 6.0 %copy-start.1 = (bf16[2,64,4,64]{3,1,2,0:T(8,128)(2,1)S(1)}, bf16[2,64,4,64]{3,1,2,0:T(8,128)(2,1)}, u32[]{:S(2)}) copy-start(bf16[2,64,4,64]{3,1,2,0:T(8,128)(2,1)} %get-tuple-element.513) | copy-start | bytes 196612 | tf_op jit(solution)/shard_map/while/body/eval_jaxpr/cond
  167.9 4.6 %copy-start.8 = (f32[128]{0:T(128)S(1)}, f32[128]{0:T(128)}, u32[]{:S(2)}) copy-start(f32[128]{0:T(128)} %get-tuple-element.743) | copy-start | bytes 1540 | tf_op jit(solution)/shard_map/while/body/eval_jaxpr/cond
  175.3 15.5 %copy-start.5 = (f32[32]{0:T(128)S(1)}, f32[32]{0:T(128)}, u32[]{:S(2)}) copy-start(f32[32]{0:T(128)} %copy-done.4) | copy-start | bytes 388 | tf_op jit(solution)/shard_map/while
  175.3 15.5 %copy-start.7 = (s32[64]{0:T(128)S(1)}, s32[64]{0:T(128)}, u32[]{:S(2)}) copy-start(s32[64]{0:T(128)} %copy-done.6) | copy-start | bytes 772 | tf_op jit(solution)/shard_map/while
  175.3 15.5 %copy-start.10 = (f32[128]{0:T(128)S(1)}, f32[128]{0:T(128)}, u32[]{:S(2)}) copy-start(f32[128]{0:T(128)} %copy-done.9) | copy-start | bytes 1540 | tf_op jit(solution)/shard_map/while
  175.3 15.5 %collective-permute-start = (bf16[128,2048]{1,0:T(8,128)(2,1)S(1)}, bf16[128,2048]{1,0:T(8,128)(2,1)S(1)}, u32[]{:S(2)}, u32[]{:S(2)}) collective-permute-start(bf16[128,2048]{1,0:T(8,128)(2,1)S(1)} %get-tuple-element.873), channel_id=1, source_target_pairs={{16,0},{17,1},{18,2},{19,3},{20,4},{21,5},{22,6},{23,7},{24,8},{25... | collective-permute-start | bytes 1572872 | tf_op jit(solution)/shard_map/while/body/eval_jaxpr/ppermute | solution.py:20
  190.8 0.6 copy-start.4
  190.8 0.6 copy-start.6
  190.8 0.6 copy-start.9
  195.9 6.0 %copy-start.1 = (bf16[2,64,4,64]{3,1,2,0:T(8,128)(2,1)S(1)}, bf16[2,64,4,64]{3,1,2,0:T(8,128)(2,1)}, u32[]{:S(2)}) copy-start(bf16[2,64,4,64]{3,1,2,0:T(8,128)(2,1)} %get-tuple-element.513) | copy-start | bytes 196612 | tf_op jit(solution)/shard_map/while/body/eval_jaxpr/cond
  203.4 4.6 %copy-start.8 = (f32[128]{0:T(128)S(1)}, f32[128]{0:T(128)}, u32[]{:S(2)}) copy-start(f32[128]{0:T(128)} %get-tuple-element.743) | copy-start | bytes 1540 | tf_op jit(solution)/shard_map/while/body/eval_jaxpr/cond
  210.8 14.6 %copy-start.5 = (f32[32]{0:T(128)S(1)}, f32[32]{0:T(128)}, u32[]{:S(2)}) copy-start(f32[32]{0:T(128)} %copy-done.4) | copy-start | bytes 388 | tf_op jit(solution)/shard_map/while
  210.8 14.6 %copy-start.7 = (s32[64]{0:T(128)S(1)}, s32[64]{0:T(128)}, u32[]{:S(2)}) copy-start(s32[64]{0:T(128)} %copy-done.6) | copy-start | bytes 772 | tf_op jit(solution)/shard_map/while
  210.8 14.6 %copy-start.10 = (f32[128]{0:T(128)S(1)}, f32[128]{0:T(128)}, u32[]{:S(2)}) copy-start(f32[128]{0:T(128)} %copy-done.9) | copy-start | bytes 1540 | tf_op jit(solution)/shard_map/while
  210.8 14.6 %collective-permute-start = (bf16[128,2048]{1,0:T(8,128)(2,1)S(1)}, bf16[128,2048]{1,0:T(8,128)(2,1)S(1)}, u32[]{:S(2)}, u32[]{:S(2)}) collective-permute-start(bf16[128,2048]{1,0:T(8,128)(2,1)S(1)} %get-tuple-element.873), channel_id=1, source_target_pairs={{16,0},{17,1},{18,2},{19,3},{20,4},{21,5},{22,6},{23,7},{24,8},{25... | collective-permute-start | bytes 1572872 | tf_op jit(solution)/shard_map/while/body/eval_jaxpr/ppermute | solution.py:20
Sparse Core Ops, SparseCore 0:
  10.8 56.6 all-gather.6
  69.6 47.9 all-gather.8
  225.6 86.6 all-reduce.4
where the time goes:
time: 323 us; the launch traced here: 322 us
  waiting for transfers between devices  178 us (55%)
  blocking collectives  41.4 us (13%)
  matrix products  33 us (10%)
  local copies, waits for them, and re-layouts  32.7 us (10%)
  other arithmetic  17.9 us (6%)
  between operations  14.6 us (5%)
  starting transfers between devices  3.99 us (1%)
    unnamed x4, waiting for transfers between devices  86.7 us
    all_gather x1, waiting for transfers between devices, per_device(): lax.all_gather(output_weight[0], 'seq', axis=0, tiled=True)  50.2 us
    ppermute x3, waiting for transfers between devices, shifted(): lax.ppermute(value, axis, [(source, source + steps) for source in range(i...  32.7 us
    all_gather x1, blocking collectives, per_device(): lax.all_gather(header_keys[0], 'seq', axis=1, tiled=True)  23.4 us
    all_gather x1, blocking collectives, per_device(): lax.all_gather(header_values[0], 'seq', axis=1, tiled=True)  18.1 us
    all_gather x1, waiting for transfers between devices, per_device(): lax.all_gather(query_weight[0], 'seq', axis=0, tiled=True)  8.04 us
    dot_general x2, matrix products, backward_rows(): jnp.einsum('nd,qd->nq', grad_output, output_full, preferred_element_type=...  7.73 us
    another operation x18, local copies, waits for them, and re-layouts  7.5 us
  transfers between devices with their start and end apart: 6, of which 6 were waited for; matrix products, arithmetic and copies ran while one was open for 11% of the time, Pallas kernels for 0%

commit v1 on v0

v1 whole, which is shorter than its diff:
```python
import functools
import math

import jax
import jax.numpy as jnp
from jax import lax
from jax.experimental import pallas as pl
from jax.experimental.pallas import tpu as pltpu
from jax.sharding import PartitionSpec as P

KEY_HEADS = 4
HEAD_WIDTH = 64
HPS = 8
GROUP = 4
LANES = GROUP * HEAD_WIDTH

EPSILON = 1e-05
ROPE_BASE = 500000.0
MESH = pl.DeviceIdType.MESH
NT = (((1,), (1,)), ((), ()))
TN = (((0,), (0,)), ((), ()))
NN = (((1,), (0,)), ((), ()))
F32 = jnp.float32
BF16 = jnp.bfloat16


def mm(a, b, dims):
    return lax.dot_general(a, b, dims, preferred_element_type=F32)


def rope_wide(positions):
    half = HEAD_WIDTH // 2
    freq_index = jnp.arange(half, dtype=F32)
    inverse = jnp.exp(freq_index * (-2.0 * math.log(ROPE_BASE) / (2 * half)))
    angles = positions.astype(F32)[..., None] * inverse
    cosine, sine = jnp.cos(angles), jnp.sin(angles)
    wide_cos = jnp.concatenate([cosine, cosine] * GROUP, axis=-1)
    wide_sin = jnp.concatenate([-sine, sine] * GROUP, axis=-1)
    return wide_cos, wide_sin


def half_swap(v):
    width = v.shape[1]
    half = HEAD_WIDTH // 2
    lane = lax.broadcasted_iota(jnp.int32, v.shape, 1)
    from_right = pltpu.roll(v, width - half, 1)
    from_left = pltpu.roll(v, half, 1)
    return jnp.where(lane % HEAD_WIDTH < half, from_right, from_left)


def rotate(v, cosine, signed_sine):
    return v * cosine + half_swap(v) * signed_sine


def fold_heads(v):
    v = v + pltpu.roll(v, 2 * HEAD_WIDTH, 1)
    return v + pltpu.roll(v, HEAD_WIDTH, 1)


def block_sum(v, ones_block):
    high = v.astype(BF16)
    low = (v - high.astype(F32)).astype(BF16)
    return mm(high, ones_block, NN) + mm(low, ones_block, NN)


def kernel(
    n, sections, *refs
):
    (
        x_ref, og_ref, gain_ref, wq_ref, wo_ref, hdr_ref, cos_ref, sin_ref, hcos_ref, hsin_ref, seg_ref,
        gi_ref, ko_ref, vo_ref,
        wq_s, wo_s, hdr_s, hd_s, kb_s, vb_s, normed_s, inv_s, q_s, p_s, gin_s, gq_s, gn_s, acc_s, part_s, rs_s,
        ssem, rsem, hs_sem, hr_sem, gs_sem, gr_sem, rss_sem, rsr_sem,
    ) = refs
    me = lax.axis_index("seq")
    sec = lax.axis_index("section")
    mbs, rows, width = x_ref.shape
    heads = hcos_ref.shape[1]
    own_heads = heads // n
    span = GROUP * heads
    line = n // 4
    a, b, c = me // 4, (me // 2) % 2, me % 2

    barrier = pltpu.get_barrier_semaphore()

    @pl.loop(1, n)
    def _(d):
        pl.semaphore_signal(barrier, inc=1, device_id={"seq": (me + d) % n}, device_id_type=MESH)

    @pl.when(sec > 0)
    def _():
        pl.semaphore_signal(barrier, inc=1, device_id={"section": sec - 1}, device_id_type=MESH)

    @pl.when(sec < sections - 1)
    def _():
        pl.semaphore_signal(barrier, inc=1, device_id={"section": sec + 1}, device_id_type=MESH)

    rq, ro = wq_ref.shape[0], wo_ref.shape[0]
    wq_s[pl.ds(pl.multiple_of(me * rq, rq), rq), :] = wq_ref[...]
    wo_s[pl.ds(pl.multiple_of(me * ro, ro), ro), :] = wo_ref[...]
    hdr_s[me] = hdr_ref[...]
    neighbours = (sec > 0).astype(jnp.int32) + (sec < sections - 1).astype(jnp.int32)
    pl.semaphore_wait(barrier, n - 1 + neighbours)

    def spot(aa, bb, cc):
        return aa * 4 + bb * 2 + cc

    def block(w, owner):
        scr, r = ((wq_s, rq), (wo_s, ro))[w]
        return scr.at[pl.ds(pl.multiple_of(owner * r, r), r), :]

    def copy(w, owner, send, recv, target):
        return pltpu.make_async_remote_copy(
            src_ref=block(w, owner),
            dst_ref=block(w, owner),
            send_sem=ssem.at[w, send[0], send[1]],
            recv_sem=rsem.at[w, recv[0], recv[1]],
            device_id={"seq": target},
            device_id_type=MESH,
        )

    def owner_line(slot):
        return a - slot if slot < line else a + (slot - line + 1)

    def valid(slot):
        if slot == 0:
            return a >= 0
        return (a >= slot) if slot < line else (a + (slot - line + 1) < line)

    def up(w, slot):
        return copy(w, spot(owner_line(slot), b, c), (0, slot), (0, slot + 1), spot(a + 1, b, c))

    def down(w, slot):
        later = line if slot == 0 else slot + 1
        return copy(w, spot(owner_line(slot), b, c), (1, slot), (0, later), spot(a - 1, b, c))

    def across(w, slot):
        return copy(w, spot(owner_line(slot), b, c), (2, slot), (1, slot), spot(a, 1 - b, c))

    def core_a(w, slot):
        return copy(w, spot(owner_line(slot), b, c), (3, slot), (2, slot), spot(a, b, 1 - c))

    def core_b(w, slot):
        return copy(w, spot(owner_line(slot), 1 - b, c), (4, slot), (3, slot), spot(a, b, 1 - c))

    def arrived(w, owner, kind, slot):
        copy(w, owner, (0, 0), (kind, slot), spot(a, b, 1 - c)).wait_recv()

    def goes_up(slot):
        return slot < line - 1

    def goes_down(slot):
        return slot == 0 or (line <= slot and slot < 2 * line - 2)

    def send_on(w, slot):
        if goes_up(slot):
            pl.when(valid(slot) & (a + 1 < line))(lambda: up(w, slot).start())
        if goes_down(slot):
            pl.when(valid(slot) & (a > 0))(lambda: down(w, slot).start())

        @pl.when(valid(slot))
        def _():
            across(w, slot).start()
            core_a(w, slot).start()

    def take_line(w, slot):
        pl.when(valid(slot))(lambda: arrived(w, spot(owner_line(slot), b, c), 0, slot))
        send_on(w, slot)

    def take_across(w, slot):
        @pl.when(valid(slot))
        def _():
            arrived(w, spot(owner_line(slot), 1 - b, c), 1, slot)
            core_b(w, slot).start()

    def take_core(w, slot):
        @pl.when(valid(slot))
        def _():
            arrived(w, spot(owner_line(slot), b, 1 - c), 2, slot)
            arrived(w, spot(owner_line(slot), 1 - b, 1 - c), 3, slot)

    def finish(w, slot):
        if goes_up(slot):
            pl.when(valid(slot) & (a + 1 < line))(lambda: up(w, slot).wait_send())
        if goes_down(slot):
            pl.when(valid(slot) & (a > 0))(lambda: down(w, slot).wait_send())

        @pl.when(valid(slot))
        def _():
            across(w, slot).wait_send()
            core_a(w, slot).wait_send()
            core_b(w, slot).wait_send()

    def slots_of(k):
        return [0] if k == 0 else [k, line - 1 + k]

    def header_copy(d):
        return pltpu.make_async_remote_copy(
            src_ref=hdr_s.at[me],
            dst_ref=hdr_s.at[me],
            send_sem=hs_sem.at[d],
            recv_sem=hr_sem.at[d],
            device_id={"seq": (me + d) % n},
            device_id_type=MESH,
        )

    def header_arrival(d):
        source = (me + n - d) % n
        return pltpu.make_async_remote_copy(
            src_ref=hdr_s.at[source],
            dst_ref=hdr_s.at[source],
            send_sem=hs_sem.at[d],
            recv_sem=hr_sem.at[d],
            device_id={"seq": (me + d) % n},
            device_id_type=MESH,
        )

    pl.loop(1, n)(lambda d: header_copy(d).start())
    for w in (0, 1):
        send_on(w, 0)

    for m in range(mbs):
        wide = x_ref[m].astype(F32)
        inv = lax.rsqrt(jnp.mean(wide * wide, axis=-1, keepdims=True) + EPSILON)
        inv_s[m] = jnp.broadcast_to(inv, (rows, 128))
        normed_s[m * rows:(m + 1) * rows, :] = (wide * inv * gain_ref[...]).astype(BF16)

    @pl.when(sec == sections - 1)
    def _():
        gin_s[...] = og_ref[...]

    pl.loop(1, n)(lambda d: header_arrival(d).wait_recv())
    for i in range(n):
        for j in range(2 * mbs):
            hd_s[j, i * own_heads:(i + 1) * own_heads, :] = hdr_s[i, j * own_heads:(j + 1) * own_heads, :]
    lane = lax.broadcasted_iota(jnp.int32, (heads, LANES), 1) // HEAD_WIDTH

    def spread(v, g):
        return fold_heads(jnp.where(lane == g, v, 0.0))

    for m in range(mbs):
        keys = rotate(hd_s[m], hcos_ref[m], hsin_ref[m]).astype(BF16).astype(F32)
        values = hd_s[mbs + m]
        for g in range(KEY_HEADS):
            wide_k, wide_v = spread(keys, g), spread(values, g)
            for j in range(GROUP):
                kb_s[m, g, j * heads:(j + 1) * heads, :] = jnp.where(lane == j, wide_k, 0.0).astype(BF16)
                vb_s[m, g, j * heads:(j + 1) * heads, :] = jnp.where(lane == j, wide_v, 0.0).astype(BF16)

    for k in range(1, line):
        for w in (0, 1):
            for slot in slots_of(k):
                take_line(w, slot)
            for slot in slots_of(k - 1):
                take_across(w, slot)
    for w in (0, 1):
        for slot in slots_of(line - 1):
            take_across(w, slot)
        for k in range(line):
            for slot in slots_of(k):
                take_core(w, slot)

    ones_block = (
        lax.broadcasted_iota(jnp.int32, (span, span), 0) // heads
        == lax.broadcasted_iota(jnp.int32, (span, span), 1) // heads
    ).astype(F32).astype(BF16)
    column = lax.broadcasted_iota(jnp.int32, (rows, span), 1)
    column_segment = (column % heads) // HPS
    cosine, sine = cos_ref[...], sin_ref[...]
    scale = HEAD_WIDTH ** (-0.5)

    @pl.loop(0, KEY_HEADS)
    def _(g):
        cols = pl.ds(pl.multiple_of(g * LANES, LANES), LANES)
        wide_cols = pl.ds(pl.multiple_of(g * span, 128), span)
        projected = mm(normed_s[...], wq_s[:, cols], NN)
        for m in range(mbs):
            query = rotate(projected[m * rows:(m + 1) * rows], cosine, sine).astype(BF16)
            q_s[m, :, cols] = query
            score = mm(query, kb_s[m, g], NT) * scale
            segment = jnp.concatenate([seg_ref[m]] * (span // 128), axis=1)
            weight = jnp.where(segment == column_segment, jnp.exp(score), 0.0)
            p_s[m, :, wide_cols] = (weight / block_sum(weight, ones_block)).astype(BF16)

    diag = (
        lax.broadcasted_iota(jnp.int32, (span, LANES), 0) // heads
        == lax.broadcasted_iota(jnp.int32, (span, LANES), 1) // HEAD_WIDTH
    )

    def folded(product):
        kept = jnp.where(diag, product, 0.0)
        total = kept[0:heads]
        for j in range(1, GROUP):
            total = total + kept[j * heads:(j + 1) * heads]
        return fold_heads(total)

    def pass_grad(m):
        return pltpu.make_async_remote_copy(
            src_ref=gi_ref.at[m],
            dst_ref=gin_s.at[m],
            send_sem=gs_sem.at[m],
            recv_sem=gr_sem.at[m],
            device_id={"section": jnp.maximum(sec - 1, 0)},
            device_id_type=MESH,
        )

    def part_copy(m, d):
        return pltpu.make_async_remote_copy(
            src_ref=part_s.at[m, (me + d) % n],
            dst_ref=rs_s.at[m, d],
            send_sem=rss_sem.at[m, d],
            recv_sem=rsr_sem.at[m, d],
            device_id={"seq": (me + d) % n},
            device_id_type=MESH,
        )

    tile = 256
    for m in range(mbs):
        pl.when(sec < sections - 1)(lambda: pass_grad(m).wait_recv())
        acc_s[...] = jnp.zeros_like(acc_s)

        @pl.loop(0, KEY_HEADS)
        def _(g):
            cols = pl.ds(pl.multiple_of(g * LANES, LANES), LANES)
            wide_cols = pl.ds(pl.multiple_of(g * span, 128), span)
            head_grad = mm(gin_s[m], wo_s[cols, :], NT).astype(BF16)
            probs = p_s[m, :, wide_cols]
            broad = probs.astype(F32)
            grad_probs = mm(head_grad, vb_s[m, g], NT)
            row_total = block_sum(broad * grad_probs, ones_block)
            grad_scores = (broad * (grad_probs - row_total) * scale).astype(BF16)
            grad_rot = mm(grad_scores, kb_s[m, g], NN)
            gq_s[:, cols] = rotate(grad_rot, cosine, -sine).astype(BF16)
            key_part = folded(mm(grad_scores, q_s[m, :, cols], TN))
            value_part = folded(mm(probs, head_grad, TN))
            here = lane == g
            acc_s[0] = jnp.where(here, key_part, acc_s[0])
            acc_s[1] = jnp.where(here, value_part, acc_s[1])

        @pl.loop(0, width // tile)
        def _(t):
            cols = pl.ds(pl.multiple_of(t * tile, tile), tile)
            gn_s[:, cols] = mm(gq_s[...], wq_s[cols, :], NT) * gain_ref[:, cols]

        wide = x_ref[m].astype(F32)
        scaled = gn_s[...]
        inv = inv_s[m][:, 0:1]
        mean = jnp.mean(wide * scaled, axis=-1, keepdims=True)
        gi_ref[m] = (
            gin_s[m].astype(F32) + inv * scaled - wide * (inv * inv * inv * mean)
        ).astype(BF16)
        pl.when(sec > 0)(lambda: pass_grad(m).start())

        key_total = rotate(acc_s[0], hcos_ref[m], -hsin_ref[m])
        value_total = acc_s[1]
        for i in range(n):
            part_s[m, i, 0:own_heads, :] = key_total[i * own_heads:(i + 1) * own_heads]
            part_s[m, i, own_heads:2 * own_heads, :] = value_total[i * own_heads:(i + 1) * own_heads]
        pl.loop(1, n)(lambda d: part_copy(m, d).start())

    for m in range(mbs):
        pl.loop(1, n)(lambda d: part_copy(m, d).wait_recv())
        rs_s[m, 0] = part_s[m, me]
        total = jnp.sum(rs_s[m], axis=0)
        ko_ref[m] = total[0:own_heads]
        vo_ref[m] = total[own_heads:2 * own_heads]
    for m in range(mbs):
        pl.loop(1, n)(lambda d: part_copy(m, d).wait_send())
        pl.when(sec > 0)(lambda: pass_grad(m).wait_send())
    pl.loop(1, n)(lambda d: header_copy(d).wait_send())
    for w in (0, 1):
        for k in range(line):
            for slot in slots_of(k):
                finish(w, slot)


def per_device(
    section_input,
    out_grad,
    norm_gain,
    query_weight,
    output_weight,
    header_keys,
    header_values,
    header_pos,
    segment_ids,
):
    sections = lax.axis_size("section")
    n = lax.axis_size("seq")
    me = lax.axis_index("seq")
    mbs, rows, width = section_input.shape[1:]
    own_heads, kv_width = header_keys.shape[2:]
    heads = own_heads * n
    span = GROUP * heads
    qw = query_weight.shape[2]
    slots = 2 * (n // 4) - 1
    headers = jnp.concatenate(
        [header_keys[0].reshape(-1, kv_width), header_values[0].reshape(-1, kv_width)], axis=0
    ).astype(F32)
    cosine, sine = rope_wide(me * rows + jnp.arange(rows, dtype=jnp.int32))
    hcos, hsin = rope_wide(header_pos)
    segments = jnp.broadcast_to(segment_ids[:, :, None], (mbs, rows, 128))
    vmem = pl.BlockSpec(memory_space=pltpu.VMEM)
    dma = pltpu.SemaphoreType.DMA
    grads, keys, values = pl.pallas_call(
        functools.partial(kernel, n, sections),
        out_shape=(
            jax.ShapeDtypeStruct((mbs, rows, width), BF16),
            jax.ShapeDtypeStruct((mbs, own_heads, kv_width), F32),
            jax.ShapeDtypeStruct((mbs, own_heads, kv_width), F32),
        ),
        in_specs=[vmem] * 11,
        out_specs=[vmem] * 3,
        scratch_shapes=[
            pltpu.VMEM((width, qw), BF16),
            pltpu.VMEM((qw, width), BF16),
            pltpu.VMEM((n, 2 * mbs * own_heads, kv_width), F32),
            pltpu.VMEM((2 * mbs, heads, kv_width), F32),
            pltpu.VMEM((mbs, KEY_HEADS, span, LANES), BF16),
            pltpu.VMEM((mbs, KEY_HEADS, span, LANES), BF16),
            pltpu.VMEM((mbs * rows, width), BF16),
            pltpu.VMEM((mbs, rows, 128), F32),
            pltpu.VMEM((mbs, rows, qw), BF16),
            pltpu.VMEM((mbs, rows, KEY_HEADS * span), BF16),
            pltpu.VMEM((mbs, rows, width), BF16),
            pltpu.VMEM((rows, qw), BF16),
            pltpu.VMEM((rows, width), F32),
            pltpu.VMEM((2, heads, kv_width), F32),
            pltpu.VMEM((mbs, n, 2 * own_heads, kv_width), F32),
            pltpu.VMEM((mbs, n, 2 * own_heads, kv_width), F32),
            dma((2, 5, slots)),
            dma((2, 4, slots)),
            dma((n,)),
            dma((n,)),
            dma((mbs,)),
            dma((mbs,)),
            dma((mbs, n)),
            dma((mbs, n)),
        ],
        compiler_params=pltpu.CompilerParams(
            collective_id=0, has_side_effects=True, vmem_limit_bytes=56 << 20
        ),
        name="relay_backward",
    )(
        section_input[0], out_grad, norm_gain, query_weight[0], output_weight[0],
        headers, cosine, sine, hcos, hsin, segments,
    )
    return (grads[None], keys[None], values[None])


def solution(mesh):
    in_specs = (
        P("section", None, "seq", None),
        P(None, "seq", None),
        P("section", None),
        P("section", "seq", None),
        P("section", "seq", None),
        P("section", None, "seq", None),
        P("section", None, "seq", None),
        P(),
        P(None, "seq"),
    )
    out_specs = (
        P("section", None, "seq", None),
        P("section", None, "seq", None),
        P("section", None, "seq", None),
    )
    return jax.shard_map(
        per_device, mesh=mesh, in_specs=in_specs, out_specs=out_specs, check_vma=False
    )
```

time: 323 us -> 122 us (0.38)
  waiting for transfers between devices: 178 us -> 0 us
  Pallas kernels: 0 us -> 111 us
  blocking collectives: 41.4 us -> 0 us
  matrix products: 33 us -> 0 us
  local copies, waits for them, and re-layouts: 32.7 us -> 9.13 us
  other arithmetic: 17.9 us -> 1.23 us
  between operations: 14.6 us -> 0.7 us
  starting transfers between devices: 3.99 us -> 0 us
    pallas_call x0 -> x1, Pallas kernels: none -> 111 us  [per_device(): pl.pallas_call(functools.partial(kernel, n, sections), out_shape=(jax.Sha...]
    unnamed x4 -> x0, waiting for transfers between devices: 86.7 us -> none
    all_gather x2 -> x0, waiting for transfers between devices: 58.2 us -> none  [the longest x1 50.2 us: per_device(): lax.all_gather(output_weight[0], 'seq', axis=0, tiled=True)]
    all_gather x2 -> x0, blocking collectives: 41.4 us -> none  [the longest x1 23.4 us: per_device(): lax.all_gather(header_keys[0], 'seq', axis=1, tiled=True)]
    ppermute x3 -> x0, waiting for transfers between devices: 32.7 us -> none  [shifted(): lax.ppermute(value, axis, [(source, source + steps) for source in range(i...]
    dot_general x14 -> x0, matrix products: 29.2 us -> none  [the longest x2 7.73 us: backward_rows(): jnp.einsum('nd,qd->nq', grad_output, output_full, preferred_element_type=...]
    scatter-add x12 -> x0, local copies, waits for them, and re-layouts: 9.3 us -> none  [the longest x6 7.15 us: step(): key_acc = key_acc.at[slot_index].add(key_part)]
    another operation x20 -> x2, local copies, waits for them, and re-layouts: 8.2 us -> 0.02 us  [the longest x1 0.01 us: per_device(): header_values[0].reshape(-1, kv_width)]
  transfers between devices with their start and end apart: 6 -> 0, of which waited for: 6 -> 0; matrix products, arithmetic and copies ran while one was open for 11% -> 0% of each run, Pallas kernels for 0% -> 0%
where the time goes in v1:
time: 122 us
  Pallas kernels  111 us (91%)
  local copies, waits for them, and re-layouts  9.13 us (7%)
  other arithmetic  1.23 us (1%)
    pallas_call x1, Pallas kernels, per_device(): pl.pallas_call(functools.partial(kernel, n, sections), out_shape=(jax.Sha...  111 us
    unnamed x15, local copies, waits for them, and re-layouts  5.04 us

profile of v1, /device:TPU:0, one launch (start us, length us, event | category | flops | bytes accessed | tf_op | source)
XLA Modules:
  0.0 122.0 jit_solution(1240755918082700613)
XLA Ops:
  0.6 0.0 copy-start.2
  0.7 0.0 copy-start.5
  0.7 0.7 copy-done.5
  1.3 0.0 copy-done.2
  1.3 0.0 copy-start.3
  1.4 0.7 copy-done.3
  2.0 0.0 copy-start.4
  2.0 0.6 maximum_convert_fusion.refs_5_
  2.7 0.1 copy-done.4
  2.7 0.7 broadcast_in_dim.8.refs_10_
  3.5 0.3 multiply_sine_fusion
  3.8 0.8 concatenate.19.refs_9_
  4.6 0.8 concatenate.18.refs_8_
  5.5 0.3 multiply_sine_fusion.1
  5.8 0.8 concatenate.17.refs_7_
  6.6 0.8 concatenate.16.refs_6_
  7.4 110.9 %relay_backward.1 = (bf16[2,128,2048]{2,1,0:T(8,128)(2,1)}, f32[2,4,256]{2,1,0:T(4,128)}, f32[2,4,256]{2,1,0:T(4,128)}) custom-call(bf16[2,128,2048]{2,1,0:T(8,128)(2,1)} %bitcast.6, bf16[2,128,2048]{2,1,0:T(8,128)(2,1)} %refs_1_.1, f32[1,2048]{1,0:T(1,128)} %refs_2_.1, bf16[128,1024]{1,0:T(8,128)(2,1)} %bitcast.8, bf16[64,2048]{1,0:T(8,128)(2,1)} %bitcast.9, ...), custom_call_target="tpu_custom_call" | custom-call | tf_op jit(solution)/shard_map/relay_backward/pallas_call | solution.py:405
  118.4 0.0 copy-start.1
  118.4 2.3 %copy.16 = bf16[1,2,128,2048]{3,2,1,0:T(8,128)(2,1)} copy(bf16[1,2,128,2048]{3,2,1,0:T(8,128)(2,1)} %bitcast.7) | data formatting | bytes 2097152
  120.7 0.0 copy-done.1
  120.7 0.0 copy-start
  120.7 0.6 copy.17
  121.3 0.1 copy-done
  121.4 0.6 copy.18
  (5 shorter events, 0.0 us)
Async XLA Ops:
  0.6 0.7 copy-start.2
  0.7 0.7 copy-start.5
  1.3 0.7 copy-start.3
  2.0 0.7 copy-start.4
  118.4 2.3 %copy-start.1 = (f32[2,4,256]{2,1,0:T(4,128)S(1)}, f32[2,4,256]{2,1,0:T(4,128)}, u32[]{:S(2)}) copy-start(f32[2,4,256]{2,1,0:T(4,128)} %get-tuple-element.7) | copy-start | bytes 24580
  120.7 0.7 copy-start

commit v2 on v1

--- a/solution.py
+++ b/solution.py
@@ -28,15 +28,20 @@
     return lax.dot_general(a, b, dims, preferred_element_type=F32)
 
 
+def as_column(row):
+    k = row.shape[1]
+    same = lax.broadcasted_iota(jnp.int32, (k, k), 0) == lax.broadcasted_iota(jnp.int32, (k, k), 1)
+    return jnp.sum(jnp.where(same, row, 0.0), axis=1, keepdims=True)
+
+
 def rope_wide(positions):
     half = HEAD_WIDTH // 2
-    freq_index = jnp.arange(half, dtype=F32)
-    inverse = jnp.exp(freq_index * (-2.0 * math.log(ROPE_BASE) / (2 * half)))
-    angles = positions.astype(F32)[..., None] * inverse
+    lane = lax.broadcasted_iota(jnp.int32, (positions.shape[0], 128), 1)
+    inverse = jnp.exp((lane % half).astype(F32) * (-2.0 * math.log(ROPE_BASE) / (2 * half)))
+    angles = positions * inverse
     cosine, sine = jnp.cos(angles), jnp.sin(angles)
-    wide_cos = jnp.concatenate([cosine, cosine] * GROUP, axis=-1)
-    wide_sin = jnp.concatenate([-sine, sine] * GROUP, axis=-1)
-    return wide_cos, wide_sin
+    sine = jnp.where(lane % HEAD_WIDTH < half, -sine, sine)
+    return jnp.concatenate([cosine] * (LANES // 128), axis=1), jnp.concatenate([sine] * (LANES // 128), axis=1)
 
 
 def half_swap(v):
@@ -67,15 +72,15 @@
     n, sections, *refs
 ):
     (
-        x_ref, og_ref, gain_ref, wq_ref, wo_ref, hdr_ref, cos_ref, sin_ref, hcos_ref, hsin_ref, seg_ref,
+        x_ref, og_ref, gain_ref, wq_ref, wo_ref, hk_ref, hv_ref, pos_ref, seg_ref,
         gi_ref, ko_ref, vo_ref,
-        wq_s, wo_s, hdr_s, hd_s, kb_s, vb_s, normed_s, inv_s, q_s, p_s, gin_s, gq_s, gn_s, acc_s, part_s, rs_s,
+        wq_s, wo_s, hdr_s, hd_s, kb_s, vb_s, normed_s, inv_s, cos_s, sin_s, hcos_s, hsin_s, q_s, p_s, gin_s, gq_s, gn_s, acc_s, part_s, rs_s,
         ssem, rsem, hs_sem, hr_sem, gs_sem, gr_sem, rss_sem, rsr_sem,
     ) = refs
     me = lax.axis_index("seq")
     sec = lax.axis_index("section")
     mbs, rows, width = x_ref.shape
-    heads = hcos_ref.shape[1]
+    heads = pos_ref.shape[1]
     own_heads = heads // n
     span = GROUP * heads
     line = n // 4
@@ -98,7 +103,8 @@
     rq, ro = wq_ref.shape[0], wo_ref.shape[0]
     wq_s[pl.ds(pl.multiple_of(me * rq, rq), rq), :] = wq_ref[...]
     wo_s[pl.ds(pl.multiple_of(me * ro, ro), ro), :] = wo_ref[...]
-    hdr_s[me] = hdr_ref[...]
+    own_headers = [hk_ref[m].astype(F32) for m in range(mbs)] + [hv_ref[m].astype(F32) for m in range(mbs)]
+    hdr_s[me] = jnp.concatenate(own_headers, axis=0)
     neighbours = (sec > 0).astype(jnp.int32) + (sec < sections - 1).astype(jnp.int32)
     pl.semaphore_wait(barrier, n - 1 + neighbours)
 
@@ -229,6 +235,12 @@
     def _():
         gin_s[...] = og_ref[...]
 
+    cos_s[...], sin_s[...] = rope_wide(
+        (me * rows + lax.broadcasted_iota(jnp.int32, (rows, 1), 0)).astype(F32)
+    )
+    for m in range(mbs):
+        hcos_s[m], hsin_s[m] = rope_wide(as_column(pos_ref[m:m + 1, :].astype(F32)))
+
     pl.loop(1, n)(lambda d: header_arrival(d).wait_recv())
     for i in range(n):
         for j in range(2 * mbs):
@@ -239,7 +251,7 @@
         return fold_heads(jnp.where(lane == g, v, 0.0))
 
     for m in range(mbs):
-        keys = rotate(hd_s[m], hcos_ref[m], hsin_ref[m]).astype(BF16).astype(F32)
+        keys = rotate(hd_s[m], hcos_s[m], hsin_s[m]).astype(BF16).astype(F32)
         values = hd_s[mbs + m]
         for g in range(KEY_HEADS):
             wide_k, wide_v = spread(keys, g), spread(values, g)
@@ -247,40 +259,54 @@
                 kb_s[m, g, j * heads:(j + 1) * heads, :] = jnp.where(lane == j, wide_k, 0.0).astype(BF16)
                 vb_s[m, g, j * heads:(j + 1) * heads, :] = jnp.where(lane == j, wide_v, 0.0).astype(BF16)
 
-    for k in range(1, line):
-        for w in (0, 1):
-            for slot in slots_of(k):
-                take_line(w, slot)
-            for slot in slots_of(k - 1):
-                take_across(w, slot)
-    for w in (0, 1):
-        for slot in slots_of(line - 1):
-            take_across(w, slot)
-        for k in range(line):
-            for slot in slots_of(k):
-                take_core(w, slot)
-
     ones_block = (
         lax.broadcasted_iota(jnp.int32, (span, span), 0) // heads
         == lax.broadcasted_iota(jnp.int32, (span, span), 1) // heads
     ).astype(F32).astype(BF16)
     column = lax.broadcasted_iota(jnp.int32, (rows, span), 1)
     column_segment = (column % heads) // HPS
-    cosine, sine = cos_ref[...], sin_ref[...]
+    cosine, sine = cos_s[...], sin_s[...]
+    segment_columns = [as_column(seg_ref[m:m + 1, :].astype(F32)).astype(jnp.int32) for m in range(mbs)]
     scale = HEAD_WIDTH ** (-0.5)
 
-    @pl.loop(0, KEY_HEADS)
-    def _(g):
-        cols = pl.ds(pl.multiple_of(g * LANES, LANES), LANES)
-        wide_cols = pl.ds(pl.multiple_of(g * span, 128), span)
+    def forward(g):
+        cols = slice(g * LANES, (g + 1) * LANES)
         projected = mm(normed_s[...], wq_s[:, cols], NN)
         for m in range(mbs):
             query = rotate(projected[m * rows:(m + 1) * rows], cosine, sine).astype(BF16)
             q_s[m, :, cols] = query
             score = mm(query, kb_s[m, g], NT) * scale
-            segment = jnp.concatenate([seg_ref[m]] * (span // 128), axis=1)
-            weight = jnp.where(segment == column_segment, jnp.exp(score), 0.0)
-            p_s[m, :, wide_cols] = (weight / block_sum(weight, ones_block)).astype(BF16)
+            weight = jnp.where(segment_columns[m] == column_segment, jnp.exp(score), 0.0)
+            p_s[m, :, g * span:(g + 1) * span] = (weight / block_sum(weight, ones_block)).astype(BF16)
+
+    def relay(w, k):
+        for slot in slots_of(k):
+            take_line(w, slot)
+        for slot in slots_of(k - 1):
+            take_across(w, slot)
+
+    def last_across(w):
+        for slot in slots_of(line - 1):
+            take_across(w, slot)
+
+    def all_core(w):
+        for k in range(line):
+            for slot in slots_of(k):
+                take_core(w, slot)
+
+    for k in range(1, line):
+        relay(0, k)
+        if k > 1:
+            relay(1, k - 1)
+    last_across(0)
+    all_core(0)
+    forward(0)
+    relay(1, line - 1)
+    forward(1)
+    last_across(1)
+    for g in range(2, KEY_HEADS):
+        forward(g)
+    all_core(1)
 
     diag = (
         lax.broadcasted_iota(jnp.int32, (span, LANES), 0) // heads
@@ -314,15 +340,22 @@
             device_id_type=MESH,
         )
 
+    def scatter(m):
+        key_total = rotate(acc_s[0], hcos_s[m], -hsin_s[m])
+        value_total = acc_s[1]
+        for i in range(n):
+            part_s[m, i, 0:own_heads, :] = key_total[i * own_heads:(i + 1) * own_heads]
+            part_s[m, i, own_heads:2 * own_heads, :] = value_total[i * own_heads:(i + 1) * own_heads]
+        pl.loop(1, n)(lambda d: part_copy(m, d).start())
+
     tile = 256
     for m in range(mbs):
         pl.when(sec < sections - 1)(lambda: pass_grad(m).wait_recv())
         acc_s[...] = jnp.zeros_like(acc_s)
 
-        @pl.loop(0, KEY_HEADS)
-        def _(g):
-            cols = pl.ds(pl.multiple_of(g * LANES, LANES), LANES)
-            wide_cols = pl.ds(pl.multiple_of(g * span, 128), span)
+        for g in range(KEY_HEADS):
+            cols = slice(g * LANES, (g + 1) * LANES)
+            wide_cols = slice(g * span, (g + 1) * span)
             head_grad = mm(gin_s[m], wo_s[cols, :], NT).astype(BF16)
             probs = p_s[m, :, wide_cols]
             broad = probs.astype(F32)
@@ -337,9 +370,11 @@
             acc_s[0] = jnp.where(here, key_part, acc_s[0])
             acc_s[1] = jnp.where(here, value_part, acc_s[1])
 
-        @pl.loop(0, width // tile)
-        def _(t):
-            cols = pl.ds(pl.multiple_of(t * tile, tile), tile)
+        if m == mbs - 1:
+            scatter(m)
+
+        for t in range(width // tile):
+            cols = slice(t * tile, (t + 1) * tile)
             gn_s[:, cols] = mm(gq_s[...], wq_s[cols, :], NT) * gain_ref[:, cols]
 
         wide = x_ref[m].astype(F32)
@@ -350,13 +385,8 @@
             gin_s[m].astype(F32) + inv * scaled - wide * (inv * inv * inv * mean)
         ).astype(BF16)
         pl.when(sec > 0)(lambda: pass_grad(m).start())
-
-        key_total = rotate(acc_s[0], hcos_ref[m], -hsin_ref[m])
-        value_total = acc_s[1]
-        for i in range(n):
-            part_s[m, i, 0:own_heads, :] = key_total[i * own_heads:(i + 1) * own_heads]
-            part_s[m, i, own_heads:2 * own_heads, :] = value_total[i * own_heads:(i + 1) * own_heads]
-        pl.loop(1, n)(lambda d: part_copy(m, d).start())
+        if m < mbs - 1:
+            scatter(m)
 
     for m in range(mbs):
         pl.loop(1, n)(lambda d: part_copy(m, d).wait_recv())
@@ -387,19 +417,12 @@
 ):
     sections = lax.axis_size("section")
     n = lax.axis_size("seq")
-    me = lax.axis_index("seq")
     mbs, rows, width = section_input.shape[1:]
     own_heads, kv_width = header_keys.shape[2:]
     heads = own_heads * n
     span = GROUP * heads
     qw = query_weight.shape[2]
     slots = 2 * (n // 4) - 1
-    headers = jnp.concatenate(
-        [header_keys[0].reshape(-1, kv_width), header_values[0].reshape(-1, kv_width)], axis=0
-    ).astype(F32)
-    cosine, sine = rope_wide(me * rows + jnp.arange(rows, dtype=jnp.int32))
-    hcos, hsin = rope_wide(header_pos)
-    segments = jnp.broadcast_to(segment_ids[:, :, None], (mbs, rows, 128))
     vmem = pl.BlockSpec(memory_space=pltpu.VMEM)
     dma = pltpu.SemaphoreType.DMA
     grads, keys, values = pl.pallas_call(
@@ -409,7 +432,7 @@
             jax.ShapeDtypeStruct((mbs, own_heads, kv_width), F32),
             jax.ShapeDtypeStruct((mbs, own_heads, kv_width), F32),
         ),
-        in_specs=[vmem] * 11,
+        in_specs=[vmem] * 9,
         out_specs=[vmem] * 3,
         scratch_shapes=[
             pltpu.VMEM((width, qw), BF16),
@@ -420,6 +443,10 @@
             pltpu.VMEM((mbs, KEY_HEADS, span, LANES), BF16),
             pltpu.VMEM((mbs * rows, width), BF16),
             pltpu.VMEM((mbs, rows, 128), F32),
+            pltpu.VMEM((rows, LANES), F32),
+            pltpu.VMEM((rows, LANES), F32),
+            pltpu.VMEM((mbs, heads, LANES), F32),
+            pltpu.VMEM((mbs, heads, LANES), F32),
             pltpu.VMEM((mbs, rows, qw), BF16),
             pltpu.VMEM((mbs, rows, KEY_HEADS * span), BF16),
             pltpu.VMEM((mbs, rows, width), BF16),
@@ -443,7 +470,7 @@
         name="relay_backward",
     )(
         section_input[0], out_grad, norm_gain, query_weight[0], output_weight[0],
-        headers, cosine, sine, hcos, hsin, segments,
+        header_keys[0], header_values[0], header_pos, segment_ids,
     )
     return (grads[None], keys[None], values[None])
 

time: 122 us -> 109 us (0.89)
  Pallas kernels: 111 us -> 105 us
  local copies, waits for them, and re-layouts: 9.13 us -> 3.61 us
  other arithmetic: 1.23 us -> 0 us
    pallas_call x1, Pallas kernels: 111 us -> 105 us  [per_device(): pl.pallas_call(functools.partial(kernel, n, sections), out_shape=(jax.Sha...]
    concatenate x4 -> x0, local copies, waits for them, and re-layouts: 3.32 us -> none  [the longest x2 1.67 us: rope_wide(): wide_sin = jnp.concatenate([-sine, sine] * GROUP, axis=-1)]
    unnamed x15 -> x7, local copies, waits for them, and re-layouts: 5.04 us -> 3.61 us
where the time goes in v2:
time: 109 us
  Pallas kernels  105 us (96%)
  local copies, waits for them, and re-layouts  3.61 us (3%)
    pallas_call x1, Pallas kernels, per_device(): pl.pallas_call(functools.partial(kernel, n, sections), out_shape=(jax.Sha...  105 us
    unnamed x7, local copies, waits for them, and re-layouts  3.61 us

profile of v2, /device:TPU:0, one launch (start us, length us, event | category | flops | bytes accessed | tf_op | source)
XLA Modules:
  0.0 109.2 jit_solution(16643450910265539961)
XLA Ops:
  0.6 104.9 %relay_backward.1 = (bf16[2,128,2048]{2,1,0:T(8,128)(2,1)}, f32[2,4,256]{2,1,0:T(4,128)}, f32[2,4,256]{2,1,0:T(4,128)}) custom-call(bf16[2,128,2048]{2,1,0:T(8,128)(2,1)} %bitcast.8, bf16[2,128,2048]{2,1,0:T(8,128)(2,1)} %refs_1_.1, f32[1,2048]{1,0:T(1,128)} %refs_2_.1, bf16[128,1024]{1,0:T(8,128)(2,1)} %bitcast.10, bf16[64,2048]{1,0:T(8,128)(2,1)} %bitcast.11, ...), custom_call_target="tpu_custom_call" | custom-call | tf_op jit(solution)/shard_map/relay_backward/pallas_call | solution.py:428
  105.5 0.0 copy-start.1
  105.6 2.3 %copy.15 = bf16[1,2,128,2048]{3,2,1,0:T(8,128)(2,1)} copy(bf16[1,2,128,2048]{3,2,1,0:T(8,128)(2,1)} %bitcast.9) | data formatting | bytes 2097152
  107.9 0.0 copy-done.1
  107.9 0.0 copy-start
  107.9 0.6 copy.16
  108.5 0.1 copy-done
  108.6 0.6 copy.17
Async XLA Ops:
  105.5 2.3 %copy-start.1 = (f32[2,4,256]{2,1,0:T(4,128)S(1)}, f32[2,4,256]{2,1,0:T(4,128)}, u32[]{:S(2)}) copy-start(f32[2,4,256]{2,1,0:T(4,128)} %get-tuple-element.7) | copy-start | bytes 24580
  107.9 0.7 copy-start

commit v3 on v2

--- a/solution.py
+++ b/solution.py
@@ -225,39 +225,42 @@
     for w in (0, 1):
         send_on(w, 0)
 
-    for m in range(mbs):
-        wide = x_ref[m].astype(F32)
-        inv = lax.rsqrt(jnp.mean(wide * wide, axis=-1, keepdims=True) + EPSILON)
-        inv_s[m] = jnp.broadcast_to(inv, (rows, 128))
-        normed_s[m * rows:(m + 1) * rows, :] = (wide * inv * gain_ref[...]).astype(BF16)
-
-    @pl.when(sec == sections - 1)
-    def _():
-        gin_s[...] = og_ref[...]
-
-    cos_s[...], sin_s[...] = rope_wide(
-        (me * rows + lax.broadcasted_iota(jnp.int32, (rows, 1), 0)).astype(F32)
-    )
-    for m in range(mbs):
-        hcos_s[m], hsin_s[m] = rope_wide(as_column(pos_ref[m:m + 1, :].astype(F32)))
-
-    pl.loop(1, n)(lambda d: header_arrival(d).wait_recv())
-    for i in range(n):
-        for j in range(2 * mbs):
-            hd_s[j, i * own_heads:(i + 1) * own_heads, :] = hdr_s[i, j * own_heads:(j + 1) * own_heads, :]
     lane = lax.broadcasted_iota(jnp.int32, (heads, LANES), 1) // HEAD_WIDTH
 
-    def spread(v, g):
-        return fold_heads(jnp.where(lane == g, v, 0.0))
-
-    for m in range(mbs):
-        keys = rotate(hd_s[m], hcos_s[m], hsin_s[m]).astype(BF16).astype(F32)
-        values = hd_s[mbs + m]
-        for g in range(KEY_HEADS):
-            wide_k, wide_v = spread(keys, g), spread(values, g)
-            for j in range(GROUP):
-                kb_s[m, g, j * heads:(j + 1) * heads, :] = jnp.where(lane == j, wide_k, 0.0).astype(BF16)
-                vb_s[m, g, j * heads:(j + 1) * heads, :] = jnp.where(lane == j, wide_v, 0.0).astype(BF16)
+    def prepare_rows():
+        for m in range(mbs):
+            wide = x_ref[m].astype(F32)
+            inv = lax.rsqrt(jnp.mean(wide * wide, axis=-1, keepdims=True) + EPSILON)
+            inv_s[m] = jnp.broadcast_to(inv, (rows, 128))
+            normed_s[m * rows:(m + 1) * rows, :] = (wide * inv * gain_ref[...]).astype(BF16)
+
+        @pl.when(sec == sections - 1)
+        def _():
+            gin_s[...] = og_ref[...]
+
+    def prepare_headers():
+        cos_s[...], sin_s[...] = rope_wide(
+            (me * rows + lax.broadcasted_iota(jnp.int32, (rows, 1), 0)).astype(F32)
+        )
+        for m in range(mbs):
+            hcos_s[m], hsin_s[m] = rope_wide(as_column(pos_ref[m:m + 1, :].astype(F32)))
+
+        pl.loop(1, n)(lambda d: header_arrival(d).wait_recv())
+        for i in range(n):
+            for j in range(2 * mbs):
+                hd_s[j, i * own_heads:(i + 1) * own_heads, :] = hdr_s[i, j * own_heads:(j + 1) * own_heads, :]
+
+        def spread(v, g):
+            return fold_heads(jnp.where(lane == g, v, 0.0))
+
+        for m in range(mbs):
+            keys = rotate(hd_s[m], hcos_s[m], hsin_s[m]).astype(BF16).astype(F32)
+            values = hd_s[mbs + m]
+            for g in range(KEY_HEADS):
+                wide_k, wide_v = spread(keys, g), spread(values, g)
+                for j in range(GROUP):
+                    kb_s[m, g, j * heads:(j + 1) * heads, :] = jnp.where(lane == j, wide_k, 0.0).astype(BF16)
+                    vb_s[m, g, j * heads:(j + 1) * heads, :] = jnp.where(lane == j, wide_v, 0.0).astype(BF16)
 
     ones_block = (
         lax.broadcasted_iota(jnp.int32, (span, span), 0) // heads
@@ -265,7 +268,6 @@
     ).astype(F32).astype(BF16)
     column = lax.broadcasted_iota(jnp.int32, (rows, span), 1)
     column_segment = (column % heads) // HPS
-    cosine, sine = cos_s[...], sin_s[...]
     segment_columns = [as_column(seg_ref[m:m + 1, :].astype(F32)).astype(jnp.int32) for m in range(mbs)]
     scale = HEAD_WIDTH ** (-0.5)
 
@@ -294,12 +296,16 @@
             for slot in slots_of(k):
                 take_core(w, slot)
 
+    prepare_rows()
     for k in range(1, line):
         relay(0, k)
         if k > 1:
             relay(1, k - 1)
+        if k == 2:
+            prepare_headers()
     last_across(0)
     all_core(0)
+    cosine, sine = cos_s[...], sin_s[...]
     forward(0)
     relay(1, line - 1)
     forward(1)

time: 109 us -> 109 us (level)
  no operation moved by 1% of the time
where the time goes in v3:
time: 109 us
  Pallas kernels  105 us (96%)
  local copies, waits for them, and re-layouts  3.61 us (3%)
    pallas_call x1, Pallas kernels, per_device(): pl.pallas_call(functools.partial(kernel, n, sections), out_shape=(jax.Sha...  105 us
    unnamed x7, local copies, waits for them, and re-layouts  3.61 us

profile of v3, /device:TPU:0, one launch (start us, length us, event | category | flops | bytes accessed | tf_op | source)
XLA Modules:
  0.0 109.2 jit_solution(11099317661041402762)
XLA Ops:
  0.6 104.9 %relay_backward.1 = (bf16[2,128,2048]{2,1,0:T(8,128)(2,1)}, f32[2,4,256]{2,1,0:T(4,128)}, f32[2,4,256]{2,1,0:T(4,128)}) custom-call(bf16[2,128,2048]{2,1,0:T(8,128)(2,1)} %bitcast.8, bf16[2,128,2048]{2,1,0:T(8,128)(2,1)} %refs_1_.1, f32[1,2048]{1,0:T(1,128)} %refs_2_.1, bf16[128,1024]{1,0:T(8,128)(2,1)} %bitcast.10, bf16[64,2048]{1,0:T(8,128)(2,1)} %bitcast.11, ...), custom_call_target="tpu_custom_call" | custom-call | tf_op jit(solution)/shard_map/relay_backward/pallas_call | solution.py:434
  105.5 0.0 copy-start.1
  105.5 2.3 %copy.15 = bf16[1,2,128,2048]{3,2,1,0:T(8,128)(2,1)} copy(bf16[1,2,128,2048]{3,2,1,0:T(8,128)(2,1)} %bitcast.9) | data formatting | bytes 2097152
  107.8 0.0 copy-done.1
  107.9 0.0 copy-start
  107.9 0.6 copy.16
  108.5 0.1 copy-done
  108.6 0.6 copy.17
Async XLA Ops:
  105.5 2.3 %copy-start.1 = (f32[2,4,256]{2,1,0:T(4,128)S(1)}, f32[2,4,256]{2,1,0:T(4,128)}, u32[]{:S(2)}) copy-start(f32[2,4,256]{2,1,0:T(4,128)} %get-tuple-element.7) | copy-start | bytes 24580
  107.9 0.7 copy-start
